TPU v7x, 128 devices: a whole 4x4x4 slice. The times are simulated.
128 devices in a mesh: rep: 16 (over y, z), grp: 8 (over x, core).
Axes of the slice: x: 4, y: 4, z: 4, core: 2. Of those that a mesh axis runs over, the one named last changes fastest.
Arguments:
- grad_query: float32 [16, 2048, 2048], P('rep', 'grp'), may hold values from -100 to 100, as said below
- error_query: float32 [16, 2048, 2048], P('rep', 'grp'), may hold values from -3 to 3
- basis_query: float32 [2048, 32], replicated, may hold values from -0.125 to 0.125
- momentum_query: float32 [2048, 2048], P('grp'), may hold values from -0.6 to 0.6
- master_query: float32 [2048, 2048], P('grp'), may hold values from -6 to 6
- grad_gate: float32 [16, 2048, 256], P('rep', 'grp'), may hold values from -100 to 100, as said below
- error_gate: float32 [16, 2048, 256], P('rep', 'grp'), may hold values from -3 to 3
- basis_gate: float32 [256, 32], replicated, may hold values from -0.375 to 0.375
- momentum_gate: float32 [2048, 256], P('grp'), may hold values from -0.6 to 0.6
- master_gate: float32 [2048, 256], P('grp'), may hold values from -6 to 6
- vector_grad: float32 [16, 12800], P('rep', 'grp'), may hold values from -6 to 6
- vector_momentum: float32 [12800], P('grp'), may hold values from -0.6 to 0.6
- vector_master: float32 [12800], P('grp'), may hold values from 0.5 to 1.5
Outputs:
- new_error_query: float32 [16, 2048, 2048], P('rep', 'grp')
- new_momentum_query: float32 [2048, 2048], P('grp')
- new_master_query: float32 [2048, 2048], P('grp')
- weight_query: bfloat16 [2048, 2048], replicated
- new_basis_query: float32 [2048, 32], replicated
- new_error_gate: float32 [16, 2048, 256], P('rep', 'grp')
- new_momentum_gate: float32 [2048, 256], P('grp')
- new_master_gate: float32 [2048, 256], P('grp')
- weight_gate: bfloat16 [2048, 256], replicated
- new_basis_gate: float32 [256, 32], replicated
- new_vector_momentum: float32 [12800], P('grp')
- new_vector_master: float32 [12800], P('grp')
- weight_vector: bfloat16 [12800], replicated
Inputs may be any that keep to these rules, and one draw needn't show every extreme that they name: `grad_query`: each replica's gradient is a common part plus a replica's own part. `grad_gate`: each replica's gradient is a common part plus a replica's own part.
All inputs are finite; a program needn't handle non-finite values.
Results may differ from a plain program's by a relative error of at most 0.0006.
Values may be sent and summed in bfloat16 or wider, within the bound.
A program may use at most 128 MiB of HBM per device.

v0:
```python
import jax
import jax.numpy as jnp
from jax import lax
from jax.sharding import PartitionSpec as P

NS_STEPS = 4
highest = lax.Precision.HIGHEST


def inverse_root(gram_matrix):
    trace_value = jnp.trace(gram_matrix)
    identity = jnp.eye(gram_matrix.shape[0], dtype=jnp.float32)
    root_part = gram_matrix / trace_value
    inverse_part = identity
    for iteration in range(NS_STEPS):
        middle = 0.5 * (3.0 * identity - jnp.dot(inverse_part, root_part, precision=highest))
        root_part = jnp.dot(root_part, middle, precision=highest)
        inverse_part = jnp.dot(middle, inverse_part, precision=highest)
    return inverse_part / jnp.sqrt(trace_value)


def right_terms(merged, ortho):
    return jnp.einsum("dn,dr->nr", merged, ortho, precision=highest)


def finish(merged, ortho, new_basis, momentum, master, replicas):
    approx = jnp.dot(ortho, new_basis.T, precision=highest) / replicas
    new_error = (merged - approx)[None]
    new_momentum = 0.9 * momentum + approx
    new_master = master - 0.5 * new_momentum
    return (new_error, new_momentum, new_master)


def per_device(
    grad_query,
    error_query,
    basis_query,
    momentum_query,
    master_query,
    grad_gate,
    error_gate,
    basis_gate,
    momentum_gate,
    master_gate,
    vector_grad,
    vector_momentum,
    vector_master,
):
    replicas = lax.axis_size("rep")
    merged_query = (grad_query + error_query)[0]
    merged_gate = (grad_gate + error_gate)[0]
    local_query = jnp.dot(merged_query, basis_query, precision=highest)
    local_gate = jnp.dot(merged_gate, basis_gate, precision=highest)
    vector_local = vector_grad[0]
    vector_total = lax.psum(vector_local, "rep")
    left_query, left_gate = lax.psum((local_query, local_gate), "rep")
    gram_query, gram_gate = lax.psum(
        (
            jnp.dot(left_query.T, left_query, precision=highest),
            jnp.dot(left_gate.T, left_gate, precision=highest),
        ),
        "grp",
    )
    ortho_query = jnp.dot(left_query, inverse_root(gram_query), precision=highest)
    ortho_gate = jnp.dot(left_gate, inverse_root(gram_gate), precision=highest)
    terms_query = right_terms(merged_query, ortho_query)
    terms_gate = right_terms(merged_gate, ortho_gate)
    basis_new_query, basis_new_gate = lax.psum((terms_query, terms_gate), ("rep", "grp"))
    error_out_query, momentum_out_query, master_out_query = finish(
        merged_query, ortho_query, basis_new_query, momentum_query, master_query, replicas
    )
    error_out_gate, momentum_out_gate, master_out_gate = finish(
        merged_gate, ortho_gate, basis_new_gate, momentum_gate, master_gate, replicas
    )
    vector_mean = vector_total / replicas
    momentum_out_vector = 0.9 * vector_momentum + vector_mean
    master_out_vector = vector_master - 0.5 * momentum_out_vector
    whole_query, whole_gate, whole_vector = (
        lax.all_gather(master_out_query.astype(jnp.bfloat16), "grp", axis=0, tiled=True),
        lax.all_gather(master_out_gate.astype(jnp.bfloat16), "grp", axis=0, tiled=True),
        lax.all_gather(master_out_vector.astype(jnp.bfloat16), "grp", axis=0, tiled=True),
    )
    return (
        error_out_query,
        momentum_out_query,
        master_out_query,
        whole_query,
        basis_new_query,
        error_out_gate,
        momentum_out_gate,
        master_out_gate,
        whole_gate,
        basis_new_gate,
        momentum_out_vector,
        master_out_vector,
        whole_vector,
    )


def solution(mesh):
    in_specs = (
        P("rep", "grp", None),
        P("rep", "grp", None),
        P(),
        P("grp", None),
        P("grp", None),
        P("rep", "grp", None),
        P("rep", "grp", None),
        P(),
        P("grp", None),
        P("grp", None),
        P("rep", "grp"),
        P("grp"),
        P("grp"),
    )
    out_specs = (
        P("rep", "grp", None),
        P("grp", None),
        P("grp", None),
        P(),
        P(),
        P("rep", "grp", None),
        P("grp", None),
        P("grp", None),
        P(),
        P(),
        P("grp"),
        P("grp"),
        P(),
    )
    return jax.shard_map(
        per_device, mesh=mesh, in_specs=in_specs, out_specs=out_specs, check_vma=False
    )
```

profile of v0, /device:TPU:1, one launch (start us, length us, event | category | flops | bytes accessed | tf_op | source)
XLA Modules:
  0.0 369.3 jit_solution(9648238144526546208)
XLA Ops:
  7.2 0.0 copy-start
  7.2 0.0 all-reduce.8.cloned.1.call-start
  7.2 1.3 reduce
  8.6 0.0 copy-start.1
  8.6 4.9 %fusion.2 = f32[256,32]{0,1:T(8,128)} fusion(f32[2048,32]{0,1:T(8,128)S(1)} %copy-done, f32[1,256,2048]{2,1,0:T(8,128)} %param.13, f32[1,256,2048]{2,1,0:T(8,128)} %param.14), kind=kOutput, calls=%fused_computation.4 | convolution fusion | flops 201850880 | bytes 4489216 | tf_op jit(solution)/shard_map/dot_general | solution.py:52
  13.5 0.0 copy-done.3
  13.5 1.0 fusion.15
  14.4 0.0 all-reduce.8.cloned.1.call-update
  14.5 0.0 all-reduce.6.cloned.1.call-start
  14.5 83.3 %all-reduce.8.cloned.1.call-done = (f32[256,32]{0,1:T(8,128)}, f32[256,32]{0,1:T(8,128)}, f32[1600]{0:T(1024)}) async-done(((f32[256,32]{0,1:T(8,128)}, f32[256,32]{0,1:T(8,128)}, f32[1600]{0:T(1024)}), (f32[256,32]{0,1:T(8,128)}, f32[256,32]{0,1:T(8,128)}, f32[1600]{0:T(1024)})) %all-reduce.8.cloned.1.call-update) | async-done | bytes 71952 | tf_op jit(solution)/shard_map/psum | solution.py:56
  97.8 1.0 fusion.29
  98.8 1.0 fusion.35
  99.8 22.7 %all-reduce.2 = (f32[32,32]{1,0:T(8,128)S(1)}, f32[32,32]{1,0:T(8,128)S(1)}) all-reduce(f32[32,32]{1,0:T(8,128)S(1)} %fusion.29, f32[32,32]{1,0:T(8,128)S(1)} %fusion.35), channel_id=1, replica_groups=mesh['rep'=16,'grp'=8] {'grp'}, use_global_device_ids=true, to_apply=%region_1.0 | all-reduce | flops 2048 | bytes 16384 | tf_op jit(solution)/shard_map/psum | solution.py:57
  122.5 0.6 select_reduce_fusion
  123.1 0.8 fusion.12
  123.9 0.1 fusion.19
  124.0 0.8 fusion.20
  124.8 0.2 fusion.11
  125.0 0.1 fusion.30
  125.1 0.1 fusion.31
  125.3 0.2 fusion.10
  125.4 0.1 fusion.32
  125.6 0.1 fusion.33
  126.5 0.8 fusion.8
  127.2 0.1 fusion.18
  127.4 0.8 fusion.21
  128.2 0.2 fusion.7
  128.3 0.1 fusion.36
  128.5 0.1 fusion.37
  128.6 0.2 fusion.6
  128.8 0.1 fusion.38
  128.9 0.1 fusion.39
  129.8 0.1 fusion.9
  129.9 0.1 convolution_divide_fusion.1
  130.1 1.0 fusion.34
  131.1 0.0 copy-done.1
  131.1 0.0 copy-start.6
  131.1 0.0 copy-start.7
  131.1 0.0 copy-start.8
  131.1 3.8 %fusion = f32[2048,32]{0,1:T(8,128)} fusion(f32[256,32]{0,1:T(8,128)S(1)} %fusion.34, f32[1,256,2048]{2,1,0:T(8,128)S(1)} %copy-done.1, f32[1,256,2048]{2,1,0:T(8,128)} %param.14), kind=kOutput, calls=%fused_computation.2 | convolution fusion | flops 201850880 | bytes 4489216 | tf_op jit(solution)/shard_map/dn,dr->nr/dot_general | solution.py:23
  134.9 0.0 all-reduce.6.cloned.1.call-update
  134.9 0.0 all-gather.5.cloned.1.call-start
  134.9 0.1 fusion.5
  135.1 0.1 convolution_divide_fusion
  135.3 0.2 fusion.40
  135.5 0.3 fusion.13
  135.8 65.4 %psum.54 = f32[256,32]{0,1:T(8,128)S(1)} all-reduce(f32[256,32]{0,1:T(8,128)S(1)} %fusion.13), channel_id=1, replica_groups=mesh['rep'=16,'grp'=8] {'rep','grp'}, use_global_device_ids=true, to_apply=%region_7.8 | all-reduce | flops 8192 | bytes 65536 | tf_op jit(solution)/shard_map/psum | solution.py:68
  201.2 1.5 fusion.27
  202.6 0.0 all-gather.5.cloned.1.call-update
  202.7 0.0 copy-start.14
  202.7 0.0 copy-start.11
  202.7 0.0 copy-start.12
  202.7 0.0 all-gather.3.cloned.1.call-start
  202.8 74.1 %all-reduce.6.cloned.1.call-done = f32[2048,32]{0,1:T(8,128)} async-done(((f32[2048,32]{0,1:T(8,128)}), f32[2048,32]{0,1:T(8,128)}) %all-reduce.6.cloned.1.call-update) | async-done | bytes 262160 | tf_op jit(solution)/shard_map/psum | solution.py:68
  276.8 8.2 %fusion.28 = (bf16[256,2048]{1,0:T(8,128)(2,1)}, f32[256,2048]{1,0:T(8,128)}, f32[256,2048]{1,0:T(8,128)}, f32[1,256,2048]{2,1,0:T(8,128)}) fusion(f32[256,2048]{1,0:T(8,128)} %param.17, f32[256,2048]{1,0:T(8,128)} %param.16, f32[1,256,2048]{2,1,0:T(8,128)S(1)} %copy-done.1, f32[1,256,2048]{2,1,0:T(8,128)} %param.14, f32[256,32]{0,1:T(8,128)S(1)} %fusion.34, ...), kind=kOutput, calls=%fused_computation.53 | convolution fusion | flops 205520896 | bytes 16023552 | tf_op jit(solution)/shard_map/dot_general | solution.py:27
  285.1 0.0 all-gather.3.cloned.1.call-update
  285.1 0.6 dynamic-slice
  286.4 0.6 fusion.26
  287.0 0.2 dynamic-update-slice
  287.3 22.5 %all-reduce = bf16[12800]{0:T(1024)(128)(2,1)} all-reduce(bf16[12800]{0:T(1024)(128)(2,1)S(1)} %dynamic-update-slice), channel_id=1, replica_groups=mesh['rep'=16,'grp'=8] {'grp'}, use_global_device_ids=true, to_apply=%add | all-reduce | flops 12800 | bytes 51200
  309.7 42.8 %all-gather.3.cloned.1.call-done = bf16[2048,2048]{1,0:T(8,128)(2,1)} async-done(((bf16[256,2048]{1,0:T(8,128)(2,1)}), bf16[2048,2048]{1,0:T(8,128)(2,1)}) %all-gather.3.cloned.1.call-update) | async-done | bytes 8388624 | tf_op jit(solution)/shard_map/all_gather | solution.py:79
  352.5 8.5 %copy.33 = bf16[2048,2048]{1,0:T(8,128)(2,1)} copy(bf16[2048,2048]{1,0:T(8,128)(2,1)} %all-gather.3.cloned.1.call-done) | data formatting | bytes 16777216
  361.1 0.7 copy.34
  361.8 1.0 copy.35
  (22 shorter events, 0.0 us)
Async XLA Ops:
  7.2 1.4 copy-start
  7.2 90.6 %all-reduce.8.cloned.1.call-start = ((), (), s32[]{:S(2)}) async-start(), calls=%async_computation.3 | async-start | bytes 147456 | tf_op jit(solution)/shard_map/psum | solution.py:56
  8.6 4.9 %copy-start.2 = (f32[1,256,256]{2,1,0:T(8,128)S(1)}, f32[1,256,256]{2,1,0:T(8,128)}, u32[]{:S(2)}) copy-start(f32[1,256,256]{2,1,0:T(8,128)} %param.18) | copy-start | bytes 786436
  8.6 4.9 %copy-start.3 = (f32[1,256,256]{2,1,0:T(8,128)S(1)}, f32[1,256,256]{2,1,0:T(8,128)}, u32[]{:S(2)}) copy-start(f32[1,256,256]{2,1,0:T(8,128)} %param.19) | copy-start | bytes 786436
  8.6 4.9 %copy-start.10 = (f32[256,32]{0,1:T(8,128)S(1)}, f32[256,32]{0,1:T(8,128)}, u32[]{:S(2)}) copy-start(f32[256,32]{0,1:T(8,128)} %param.20) | copy-start | bytes 98308
  8.6 122.5 %copy-start.1 = (f32[1,256,2048]{2,1,0:T(8,128)S(1)}, f32[1,256,2048]{2,1,0:T(8,128)}, u32[]{:S(2)}) copy-start(f32[1,256,2048]{2,1,0:T(8,128)} %param.13) | copy-start | bytes 6291460
  14.5 262.4 %all-reduce.6.cloned.1.call-start = ((), (), s32[]{:S(2)}) async-start(), calls=%async_computation | async-start | bytes 524288 | tf_op jit(solution)/shard_map/psum | solution.py:68
  131.1 4.2 %copy-start.6 = (f32[256,32]{0,1:T(8,128)S(1)}, f32[256,32]{0,1:T(8,128)}, u32[]{:S(2)}) copy-start(f32[256,32]{0,1:T(8,128)} %get-tuple-element.14) | copy-start | bytes 98308
  131.1 70.1 %copy-start.7 = (f32[256,256]{1,0:T(8,128)S(1)}, f32[256,256]{1,0:T(8,128)}, u32[]{:S(2)}) copy-start(f32[256,256]{1,0:T(8,128)} %param.22) | copy-start | bytes 786436
  131.1 70.1 %copy-start.8 = (f32[256,256]{1,0:T(8,128)S(1)}, f32[256,256]{1,0:T(8,128)}, u32[]{:S(2)}) copy-start(f32[256,256]{1,0:T(8,128)} %param.21) | copy-start | bytes 786436
  134.9 174.8 %all-gather.5.cloned.1.call-start = ((), (), s32[]{:S(2)}) async-start(), calls=%async_computation.2 | async-start | bytes 1179648 | tf_op jit(solution)/shard_map/all_gather | solution.py:80
  201.2 83.9 %copy-start.9 = (f32[256,32]{0,1:T(8,128)}, f32[256,32]{0,1:T(8,128)S(1)}, u32[]{:S(2)}) copy-start(f32[256,32]{0,1:T(8,128)S(1)} %psum.54) | copy-start | bytes 98308
  202.7 82.5 %copy-start.14 = (u32[128]{0:T(128)S(1)}, u32[128]{0:T(128)}, u32[]{:S(2)}) copy-start(u32[128]{0:T(128)} %constant.33) | copy-start | bytes 1540
  202.7 83.7 %copy-start.11 = (f32[1600]{0:T(1024)S(1)}, f32[1600]{0:T(1024)}, u32[]{:S(2)}) copy-start(f32[1600]{0:T(1024)} %param.25) | copy-start | bytes 19204
  202.7 83.7 %copy-start.12 = (f32[1600]{0:T(1024)S(1)}, f32[1600]{0:T(1024)}, u32[]{:S(2)}) copy-start(f32[1600]{0:T(1024)} %param.24) | copy-start | bytes 19204
  202.7 83.7 %copy-start.13 = (f32[1600]{0:T(1024)S(1)}, f32[1600]{0:T(1024)}, u32[]{:S(2)}) copy-start(f32[1600]{0:T(1024)} %get-tuple-element.15) | copy-start | bytes 19204
  202.7 149.8 %all-gather.3.cloned.1.call-start = ((), (), s32[]{:S(2)}) async-start(), calls=%async_computation.1 | async-start | bytes 9437184 | tf_op jit(solution)/shard_map/all_gather | solution.py:79
  352.5 8.6 %copy-start.4 = (f32[2048,32]{0,1:T(8,128)S(1)}, f32[2048,32]{0,1:T(8,128)}, u32[]{:S(2)}) copy-start(f32[2048,32]{0,1:T(8,128)} %all-reduce.6.cloned.1.call-done) | copy-start | bytes 786436
  352.5 9.3 %copy-start.5 = (bf16[2048,256]{1,0:T(8,128)(2,1)S(1)}, bf16[2048,256]{1,0:T(8,128)(2,1)}, u32[]{:S(2)}) copy-start(bf16[2048,256]{1,0:T(8,128)(2,1)} %all-gather.5.cloned.1.call-done) | copy-start | bytes 3145732
Sparse Core Ops, SparseCore 0:
  14.6 83.1 all-reduce.7
  135.0 141.7 all-reduce.5
  279.3 21.1 all-gather.4
  302.7 49.7 all-gather.2
where the time goes:
time: 370 us; the launch traced here: 369 us
  waiting for transfers between devices  200 us (54%)
  blocking collectives  111 us (30%)
  matrix products  28.5 us (8%)
  between operations  16.1 us (4%)
  local copies, waits for them, and re-layouts  11.1 us (3%)
    psum x1, waiting for transfers between devices, per_device(): left_query, left_gate = lax.psum((local_query, local_gate), 'rep')  83.3 us
    psum x1, waiting for transfers between devices, per_device(): lax.psum((terms_query, terms_gate), ('rep', 'grp'))  74.1 us
    psum x1, blocking collectives, per_device(): lax.psum((terms_query, terms_gate), ('rep', 'grp'))  65.4 us
    all_gather x1, waiting for transfers between devices, per_device(): lax.all_gather(master_out_query.astype(jnp.bfloat16), 'grp', axis=0, tile...  42.8 us
    psum x1, blocking collectives, per_device(): lax.psum((jnp.dot(left_query.T, left_query, precision=highest), jnp.dot(l...  22.7 us
    unnamed x1, blocking collectives  22.5 us
    unnamed x36, local copies, waits for them, and re-layouts  11.1 us
    dot_general x2, matrix products, finish(): approx = jnp.dot(ortho, new_basis.T, precision=highest) / replicas  9.7 us
  transfers between devices with their start and end apart: 4, of which 3 were waited for; matrix products, arithmetic and copies ran while one was open for 3% of the time, Pallas kernels for 0%

commit v1 on v0

--- a/solution.py
+++ b/solution.py
@@ -76,7 +76,15 @@
     momentum_out_vector = 0.9 * vector_momentum + vector_mean
     master_out_vector = vector_master - 0.5 * momentum_out_vector
     whole_query, whole_gate, whole_vector = (
-        lax.all_gather(master_out_query.astype(jnp.bfloat16), "grp", axis=0, tiled=True),
+        jnp.concatenate(
+            lax.all_to_all(
+                jnp.stack([master_out_query.astype(jnp.bfloat16)] * lax.axis_size("grp")),
+                "grp",
+                0,
+                0,
+            ),
+            axis=0,
+        ),
         lax.all_gather(master_out_gate.astype(jnp.bfloat16), "grp", axis=0, tiled=True),
         lax.all_gather(master_out_vector.astype(jnp.bfloat16), "grp", axis=0, tiled=True),
     )

time: 370 us -> 485 us (1.31)
  blocking collectives: 111 us -> 188 us
  waiting for transfers between devices: 200 us -> 225 us
  starting transfers between devices: 0.16 us -> 6.1 us
    psum x1, blocking collectives: 65.4 us -> 144 us  [per_device(): lax.psum((terms_query, terms_gate), ('rep', 'grp'))]
    psum x1, waiting for transfers between devices: 74.1 us -> 142 us  [per_device(): lax.psum((terms_query, terms_gate), ('rep', 'grp'))]
    all_gather x1 -> x0, waiting for transfers between devices: 42.8 us -> none  [per_device(): lax.all_gather(master_out_query.astype(jnp.bfloat16), 'grp', axis=0, tile...]
    all_to_all x0 -> x1, starting transfers between devices: none -> 5.98 us  [per_device(): lax.all_to_all(jnp.stack([master_out_query.astype(jnp.bfloat16)] * lax.ax...]
  transfers between devices with their start and end apart: 4 -> 4, of which waited for: 3 -> 2; matrix products, arithmetic and copies ran while one was open for 3% -> 1% of each run, Pallas kernels for 0% -> 0%
where the time goes in v1:
time: 485 us; the launch traced here: 482 us
  waiting for transfers between devices  225 us (46%)
  blocking collectives  188 us (39%)
  matrix products  28.1 us (6%)
  between operations  16 us (3%)
  local copies, waits for them, and re-layouts  15.6 us (3%)
  starting transfers between devices  6.1 us (1%)
    psum x1, blocking collectives, per_device(): lax.psum((terms_query, terms_gate), ('rep', 'grp'))  144 us
    psum x1, waiting for transfers between devices, per_device(): lax.psum((terms_query, terms_gate), ('rep', 'grp'))  142 us
    psum x1, waiting for transfers between devices, per_device(): left_query, left_gate = lax.psum((local_query, local_gate), 'rep')  83.3 us
    psum x1, blocking collectives, per_device(): lax.psum((jnp.dot(left_query.T, left_query, precision=highest), jnp.dot(l...  22.7 us
    unnamed x1, blocking collectives  22.1 us
    unnamed x36, local copies, waits for them, and re-layouts  11.1 us
  transfers between devices with their start and end apart: 4, of which 2 were waited for; matrix products, arithmetic and copies ran while one was open for 1% of the time, Pallas kernels for 0%

profile of v1, /device:TPU:1, one launch (start us, length us, event | category | flops | bytes accessed | tf_op | source)
XLA Modules:
  0.0 482.1 jit_solution(211546581112215759)
XLA Ops:
  7.2 0.0 copy-start
  7.2 0.0 all-reduce.8.cloned.1.call-start
  7.2 1.3 reduce
  8.6 0.0 copy-done
  8.6 0.0 copy-start.1
  8.6 4.9 %fusion.2 = f32[256,32]{0,1:T(8,128)} fusion(f32[2048,32]{0,1:T(8,128)S(1)} %copy-done, f32[1,256,2048]{2,1,0:T(8,128)} %param.13, f32[1,256,2048]{2,1,0:T(8,128)} %param.14), kind=kOutput, calls=%fused_computation.4 | convolution fusion | flops 201850880 | bytes 4489216 | tf_op jit(solution)/shard_map/dot_general | solution.py:52
  13.5 0.0 copy-done.2
  13.5 0.0 copy-done.3
  13.5 0.0 copy-done.10
  13.5 1.0 fusion.15
  14.4 0.0 all-reduce.8.cloned.1.call-update
  14.5 0.0 all-reduce.6.cloned.1.call-start
  14.5 83.3 %all-reduce.8.cloned.1.call-done = (f32[256,32]{0,1:T(8,128)}, f32[256,32]{0,1:T(8,128)}, f32[1600]{0:T(1024)}) async-done(((f32[256,32]{0,1:T(8,128)}, f32[256,32]{0,1:T(8,128)}, f32[1600]{0:T(1024)}), (f32[256,32]{0,1:T(8,128)}, f32[256,32]{0,1:T(8,128)}, f32[1600]{0:T(1024)})) %all-reduce.8.cloned.1.call-update) | async-done | bytes 71952 | tf_op jit(solution)/shard_map/psum | solution.py:56
  97.8 1.0 fusion.29
  98.8 1.0 fusion.35
  99.8 22.7 %all-reduce.2 = (f32[32,32]{1,0:T(8,128)S(1)}, f32[32,32]{1,0:T(8,128)S(1)}) all-reduce(f32[32,32]{1,0:T(8,128)S(1)} %fusion.29, f32[32,32]{1,0:T(8,128)S(1)} %fusion.35), channel_id=1, replica_groups=mesh['rep'=16,'grp'=8] {'grp'}, use_global_device_ids=true, to_apply=%region_1.0 | all-reduce | flops 2048 | bytes 16384 | tf_op jit(solution)/shard_map/psum | solution.py:57
  122.5 0.6 select_reduce_fusion
  123.1 0.8 fusion.12
  123.9 0.1 fusion.19
  124.0 0.8 fusion.20
  124.8 0.2 fusion.11
  125.0 0.1 fusion.30
  125.1 0.1 fusion.31
  125.3 0.2 fusion.10
  125.4 0.1 fusion.32
  125.6 0.1 fusion.33
  126.4 0.1 fusion.9
  126.6 0.1 convolution_divide_fusion.1
  126.7 1.0 fusion.34
  127.7 0.0 copy-done.1
  127.7 3.7 fusion
  131.4 0.0 all-reduce.6.cloned.1.call-update
  131.4 142.0 %all-reduce.6.cloned.1.call-done = f32[2048,32]{0,1:T(8,128)} async-done(((f32[2048,32]{0,1:T(8,128)}), f32[2048,32]{0,1:T(8,128)}) %all-reduce.6.cloned.1.call-update) | async-done | bytes 262160 | tf_op jit(solution)/shard_map/psum | solution.py:68
  273.4 8.0 %fusion.28 = (bf16[256,2048]{1,0:T(8,128)(2,1)S(1)}, f32[256,2048]{1,0:T(8,128)}, f32[256,2048]{1,0:T(8,128)}, f32[1,256,2048]{2,1,0:T(8,128)}) fusion(f32[256,2048]{1,0:T(8,128)} %param.17, f32[256,2048]{1,0:T(8,128)} %param.16, f32[1,256,2048]{2,1,0:T(8,128)S(1)} %copy-done.1, f32[1,256,2048]{2,1,0:T(8,128)} %param.14, f32[256,32]{0,1:T(8,128)S(1)} %fusion.34, ...), kind=kOutput, calls=%fused_computation.53 | convolution fusion | flops 205520896 | bytes 16023552 | tf_op jit(solution)/shard_map/dot_general | solution.py:27
  281.4 4.5 stack.2
  285.9 6.0 %all-to-all-start = ((bf16[8,256,2048]{2,1,0:T(8,128)(2,1)}), bf16[8,256,2048]{2,1,0:T(8,128)(2,1)}, u32[]{:S(2)}, u32[]{:S(2)}) async-start(bf16[8,256,2048]{2,1,0:T(8,128)(2,1)} %stack.2), calls=%async_computation | async-start | bytes 16777216 | tf_op jit(solution)/shard_map/all_to_all | solution.py:80
  291.9 0.0 copy-start.13
  291.9 0.0 all-gather.2.cloned.1.call-start
  292.6 0.8 fusion.8
  293.4 0.1 fusion.18
  293.5 0.8 fusion.21
  294.3 0.2 fusion.7
  294.5 0.1 fusion.36
  294.6 0.1 fusion.37
  294.8 0.2 fusion.6
  294.9 0.1 fusion.38
  295.1 0.1 fusion.39
  295.2 0.2 fusion.5
  295.4 0.1 convolution_divide_fusion
  295.6 0.0 copy-done.6
  295.6 0.2 fusion.40
  295.8 0.3 fusion.13
  296.1 143.6 %psum.54 = f32[256,32]{0,1:T(8,128)S(1)} all-reduce(f32[256,32]{0,1:T(8,128)S(1)} %fusion.13), channel_id=1, replica_groups=mesh['rep'=16,'grp'=8] {'rep','grp'}, use_global_device_ids=true, to_apply=%region_7.8 | all-reduce | flops 8192 | bytes 65536 | tf_op jit(solution)/shard_map/psum | solution.py:68
  439.7 1.4 fusion.27
  441.1 0.0 all-gather.2.cloned.1.call-update
  441.1 0.6 dynamic-slice
  442.4 0.6 fusion.26
  443.0 0.2 dynamic-update-slice
  443.3 22.1 %all-reduce = bf16[12800]{0:T(1024)(128)(2,1)} all-reduce(bf16[12800]{0:T(1024)(128)(2,1)S(1)} %dynamic-update-slice), channel_id=1, replica_groups=mesh['rep'=16,'grp'=8] {'grp'}, use_global_device_ids=true, to_apply=%add | all-reduce | flops 12800 | bytes 51200
  465.3 0.0 all-to-all-done
  465.3 8.5 %copy.33 = bf16[2048,2048]{1,0:T(8,128)(2,1)} copy(bf16[2048,2048]{1,0:T(8,128)(2,1)} %bitcast.2) | data formatting | bytes 16777216
  473.9 0.7 copy.34
  474.6 0.0 copy-done.5
  474.6 1.0 copy.35
  (22 shorter events, 0.0 us)
Async XLA Ops:
  7.2 1.4 copy-start
  7.2 90.6 %all-reduce.8.cloned.1.call-start = ((), (), s32[]{:S(2)}) async-start(), calls=%async_computation.3 | async-start | bytes 147456 | tf_op jit(solution)/shard_map/psum | solution.py:56
  8.6 4.9 %copy-start.2 = (f32[1,256,256]{2,1,0:T(8,128)S(1)}, f32[1,256,256]{2,1,0:T(8,128)}, u32[]{:S(2)}) copy-start(f32[1,256,256]{2,1,0:T(8,128)} %param.18) | copy-start | bytes 786436
  8.6 4.9 %copy-start.3 = (f32[1,256,256]{2,1,0:T(8,128)S(1)}, f32[1,256,256]{2,1,0:T(8,128)}, u32[]{:S(2)}) copy-start(f32[1,256,256]{2,1,0:T(8,128)} %param.19) | copy-start | bytes 786436
  8.6 4.9 %copy-start.10 = (f32[256,32]{0,1:T(8,128)S(1)}, f32[256,32]{0,1:T(8,128)}, u32[]{:S(2)}) copy-start(f32[256,32]{0,1:T(8,128)} %param.20) | copy-start | bytes 98308
  8.6 119.1 %copy-start.1 = (f32[1,256,2048]{2,1,0:T(8,128)S(1)}, f32[1,256,2048]{2,1,0:T(8,128)}, u32[]{:S(2)}) copy-start(f32[1,256,2048]{2,1,0:T(8,128)} %param.13) | copy-start | bytes 6291460
  14.5 259.0 %all-reduce.6.cloned.1.call-start = ((), (), s32[]{:S(2)}) async-start(), calls=%async_computation.1 | async-start | bytes 524288 | tf_op jit(solution)/shard_map/psum | solution.py:68
  285.9 9.7 %copy-start.6 = (f32[256,32]{0,1:T(8,128)S(1)}, f32[256,32]{0,1:T(8,128)}, u32[]{:S(2)}) copy-start(f32[256,32]{0,1:T(8,128)} %get-tuple-element.14) | copy-start | bytes 98308
  285.9 153.8 %copy-start.7 = (f32[256,256]{1,0:T(8,128)S(1)}, f32[256,256]{1,0:T(8,128)}, u32[]{:S(2)}) copy-start(f32[256,256]{1,0:T(8,128)} %param.22) | copy-start | bytes 786436
  285.9 153.8 %copy-start.8 = (f32[256,256]{1,0:T(8,128)S(1)}, f32[256,256]{1,0:T(8,128)}, u32[]{:S(2)}) copy-start(f32[256,256]{1,0:T(8,128)} %param.21) | copy-start | bytes 786436
  285.9 179.5 %all-to-all-start = ((bf16[8,256,2048]{2,1,0:T(8,128)(2,1)}), bf16[8,256,2048]{2,1,0:T(8,128)(2,1)}, u32[]{:S(2)}, u32[]{:S(2)}) async-start(bf16[8,256,2048]{2,1,0:T(8,128)(2,1)} %stack.2), calls=%async_computation | async-start | bytes 16777216 | tf_op jit(solution)/shard_map/all_to_all | solution.py:80
  291.8 149.3 %copy-start.14 = (u32[128]{0:T(128)S(1)}, u32[128]{0:T(128)}, u32[]{:S(2)}) copy-start(u32[128]{0:T(128)} %constant.33) | copy-start | bytes 1540
  291.8 150.5 %copy-start.11 = (f32[1600]{0:T(1024)S(1)}, f32[1600]{0:T(1024)}, u32[]{:S(2)}) copy-start(f32[1600]{0:T(1024)} %param.25) | copy-start | bytes 19204
  291.9 150.5 %copy-start.12 = (f32[1600]{0:T(1024)S(1)}, f32[1600]{0:T(1024)}, u32[]{:S(2)}) copy-start(f32[1600]{0:T(1024)} %param.24) | copy-start | bytes 19204
  291.9 150.6 %copy-start.13 = (f32[1600]{0:T(1024)S(1)}, f32[1600]{0:T(1024)}, u32[]{:S(2)}) copy-start(f32[1600]{0:T(1024)} %get-tuple-element.15) | copy-start | bytes 19204
  291.9 173.5 %all-gather.2.cloned.1.call-start = ((), (), s32[]{:S(2)}) async-start(), calls=%async_computation.2 | async-start | bytes 1179648 | tf_op jit(solution)/shard_map/all_gather | solution.py:88
  439.7 34.2 %copy-start.9 = (f32[256,32]{0,1:T(8,128)}, f32[256,32]{0,1:T(8,128)S(1)}, u32[]{:S(2)}) copy-start(f32[256,32]{0,1:T(8,128)S(1)} %psum.54) | copy-start | bytes 98308
  465.3 8.6 %copy-start.4 = (f32[2048,32]{0,1:T(8,128)S(1)}, f32[2048,32]{0,1:T(8,128)}, u32[]{:S(2)}) copy-start(f32[2048,32]{0,1:T(8,128)} %all-reduce.6.cloned.1.call-done) | copy-start | bytes 786436
  465.3 9.3 %copy-start.5 = (bf16[2048,256]{1,0:T(8,128)(2,1)S(1)}, bf16[2048,256]{1,0:T(8,128)(2,1)}, u32[]{:S(2)}) copy-start(bf16[2048,256]{1,0:T(8,128)(2,1)} %all-gather.2.cloned.1.call-done) | copy-start | bytes 3145732
Sparse Core Ops, SparseCore 0:
  14.6 83.1 all-reduce.7
  131.6 141.8 all-reduce.5
  441.3 20.4 all-gather.1
